TPU v7x, 32 devices: a whole 2x2x4 slice. The times are simulated.
32 devices in a mesh: seq: 16 (over z, x, core), res: 2 (over y).
Axes of the slice: x: 2, y: 2, z: 4, core: 2. Of those that a mesh axis runs over, the one named last changes fastest.
Arguments:
- embedded_aligned_rows: bfloat16 [48, 256, 768], P('seq', 'res'), may hold values from -12 to 12
- norm_multiplier: float32 [768], replicated, may hold values from 0.1 to 1.9
- asker_projector: bfloat16 [768, 768], replicated, may hold values from -1 to 1
- matcher_projector: bfloat16 [768, 768], replicated, may hold values from -1 to 1
- content_projector: bfloat16 [768, 768], replicated, may hold values from -0.21875 to 0.21875
- final_projector: bfloat16 [768, 768], replicated, may hold values from -0.21875 to 0.21875
Outputs:
- mixed: bfloat16 [48, 256, 768], P('seq', 'res')
All inputs are finite; a program needn't handle non-finite values.
Results may differ from a plain program's by a relative error of at most 0.01.
Values may be sent and summed in bfloat16 or wider, within the bound.
No kernel may reach another device: no remote copies, remote signals or barrier semaphores. Data moves between devices by JAX's collectives and lax.ppermute only.
A program may use at most 64 MiB of HBM per device.

v0:
```python
import jax
import jax.numpy as jnp
from jax import lax
from jax.sharding import PartitionSpec as P

HEADS = 12


def standardize_rows(embedded_aligned_rows, norm_multiplier):
    content_array = embedded_aligned_rows.astype(jnp.float32)
    center = content_array - jnp.mean(content_array, axis=-1, keepdims=True)
    spread = jnp.mean(center * center, axis=-1, keepdims=True)
    return (center / jnp.sqrt(spread + 1e-05) * norm_multiplier).astype(jnp.bfloat16)


def body(
    embedded_aligned_rows,
    norm_multiplier,
    asker_projector,
    matcher_projector,
    content_projector,
    final_projector,
):
    row_portion, column_portion, embedding_dimension = embedded_aligned_rows.shape
    heads = HEADS
    hsize = embedding_dimension // heads
    unrolled_array = standardize_rows(embedded_aligned_rows, norm_multiplier).reshape(
        row_portion * column_portion, embedding_dimension
    )
    query = jnp.dot(unrolled_array, asker_projector, preferred_element_type=jnp.float32).astype(
        jnp.bfloat16
    )
    query = query.reshape(row_portion, column_portion, heads, hsize)
    key_local = jnp.dot(
        unrolled_array, matcher_projector, preferred_element_type=jnp.float32
    ).astype(jnp.bfloat16)
    key_local = key_local.reshape(row_portion, column_portion, embedding_dimension)
    value_local = jnp.dot(
        unrolled_array, content_projector, preferred_element_type=jnp.float32
    ).astype(jnp.bfloat16)
    value_local = value_local.reshape(row_portion, column_portion, embedding_dimension)
    total_seqs = row_portion * lax.axis_size("seq")
    scale = 1.0 / (jnp.sqrt(jnp.float32(hsize)) * jnp.sqrt(jnp.float32(total_seqs)))
    key_all, value_all = (
        lax.all_gather(key_local, "res", axis=1, tiled=True),
        lax.all_gather(value_local, "res", axis=1, tiled=True),
    )
    keys = key_all.reshape(row_portion, key_all.shape[1], heads, hsize)
    logits = jnp.einsum("sihe,sjhe->hij", query, keys, preferred_element_type=jnp.float32)
    share = lax.psum_scatter(logits, "seq", scatter_dimension=1, tiled=True)
    share_probs = jax.nn.softmax(share * scale, axis=-1).astype(jnp.bfloat16)
    probs = lax.all_gather(share_probs, "seq", axis=1, tiled=True)
    content_array = value_all.reshape(row_portion, value_all.shape[1], heads, hsize)
    attended = jnp.einsum(
        "hij,sjhe->sihe", probs, content_array, preferred_element_type=jnp.float32
    )
    attended = attended.astype(jnp.bfloat16).reshape(
        row_portion * column_portion, embedding_dimension
    )
    mixed = jnp.dot(attended, final_projector, preferred_element_type=jnp.float32).astype(
        jnp.bfloat16
    )
    return mixed.reshape(row_portion, column_portion, embedding_dimension)


def solution(mesh):
    placed = (P("seq", "res", None), P(), P(), P(), P(), P())
    return jax.shard_map(
        body, mesh=mesh, in_specs=placed, out_specs=P("seq", "res", None), check_vma=False
    )
```

profile of v0, /device:TPU:0, one launch (start us, length us, event | category | flops | bytes accessed | tf_op | source)
XLA Modules:
  0.0 134.4 jit_solution(8885785728018542669)
XLA Ops:
  6.5 0.0 copy-start
  6.5 0.0 copy-start.1
  6.5 0.0 copy-start.2
  6.5 0.0 all-gather.5.cloned.1.call-start
  6.5 1.4 %convert_reduce_fusion = f32[3,128]{1,0:T(4,128)S(1)} fusion(bf16[3,128,768]{2,1,0:T(8,128)(2,1)} %param.6), kind=kLoop, calls=%fused_computation.4 | loop fusion | flops 589440 | bytes 591360 | tf_op jit(solution)/shard_map/reduce_sum | solution.py:11
  7.9 1.4 %fusion.5 = f32[3,128]{1,0:T(4,128)S(1)} fusion(bf16[3,128,768]{2,1,0:T(8,128)(2,1)} %param.6, f32[3,128]{1,0:T(4,128)S(1)} %broadcast_multiply_fusion), kind=kLoop, calls=%fused_computation.13 | loop fusion | flops 1179264 | bytes 592896 | tf_op jit(solution)/shard_map/reduce_sum | solution.py:12
  9.3 0.0 copy-done.1
  9.3 0.0 copy-done.2
  9.3 0.2 fusion.7
  9.6 0.0 copy-done
  9.6 0.6 convolution_convert_fusion.2
  10.2 0.0 copy-start.3
  10.2 1.1 copy.10
  11.3 0.0 all-gather.5.cloned.1.call-update
  11.3 0.0 reduce-scatter.2.cloned.1.call-start
  11.3 0.3 copy-done.3
  11.7 1.4 %convolution_convert_fusion.3 = bf16[384,768]{1,0:T(8,128)(2,1)} fusion(bf16[384,768]{1,0:T(8,128)(2,1)S(1)} %bitcast.33, bf16[768,768]{1,0:T(8,128)(2,1)S(1)} %copy-done.3), kind=kOutput, calls=%fused_computation.10 | convolution fusion | flops 453279744 | bytes 2359296 | tf_op jit(solution)/shard_map/dot_general | solution.py:30
  13.1 1.9 %reshape.49 = bf16[3,128,12,64]{3,2,1,0:T(8,128)(2,1)S(1)} reshape(bf16[384,768]{1,0:T(8,128)(2,1)} %convolution_convert_fusion.3) | data formatting | bytes 1179648 | tf_op jit(solution)/shard_map/reshape | solution.py:33
  15.1 21.8 %all-gather.5.cloned.1.call-done = bf16[3,256,768]{1,2,0:T(8,128)(2,1)} async-done(((bf16[3,128,768]{1,2,0:T(8,128)(2,1)}), bf16[3,256,768]{1,2,0:T(8,128)(2,1)}) %all-gather.5.cloned.1.call-update) | async-done | bytes 1179664 | tf_op jit(solution)/shard_map/all_gather | solution.py:45
  36.9 2.9 %convolution_bitcast_fusion = f32[12,128,256]{2,1,0:T(8,128)} fusion(bf16[3,128,12,64]{3,2,1,0:T(8,128)(2,1)S(1)} %reshape.49, bf16[3,256,12,64]{1,3,2,0:T(8,128)(2,1)} %bitcast.30), kind=kOutput, calls=%fused_computation.2 | convolution fusion | flops 150994944 | bytes 3342336 | tf_op jit(solution)/shard_map/sihe,sjhe->hij/dot_general | solution.py:49
  39.8 0.0 copy-start.4
  39.8 0.0 reduce-scatter.2.cloned.1.call-update
  39.8 0.0 all-gather.3.cloned.1.call-start
  39.9 1.2 copy-done.4
  41.1 0.6 convolution_convert_fusion.4
  41.7 1.1 copy.8
  42.8 0.0 all-gather.3.cloned.1.call-update
  42.8 57.4 %reduce-scatter.2.cloned.1.call-done = f32[12,8,256]{2,1,0:T(8,128)} async-done(((f32[12,128,256]{2,1,0:T(8,128)}), f32[12,8,256]{2,1,0:T(8,128)}) %reduce-scatter.2.cloned.1.call-update) | async-done | bytes 98320 | tf_op jit(solution)/shard_map/reduce_scatter | solution.py:50
  100.1 1.1 fusion.14
  101.2 21.5 %all_gather.11 = bf16[12,128,256]{2,1,0:T(8,128)(2,1)S(1)} all-gather(bf16[12,8,256]{2,1,0:T(8,128)(2,1)S(1)} %fusion.14), channel_id=1, replica_groups=mesh['seq'=16,'res'=2] {'seq'}, dimensions={1}, use_global_device_ids=true | all-gather | bytes 835584 | tf_op jit(solution)/shard_map/all_gather | solution.py:52
  122.7 0.7 all-gather.3.cloned.1.call-done
  123.4 1.7 %fusion.4 = bf16[3,128,12,64]{1,3,0,2:T(8,128)(2,1)S(1)} fusion(bf16[3,256,12,64]{1,3,2,0:T(8,128)(2,1)} %bitcast.37, bf16[12,128,256]{2,1,0:T(8,128)(2,1)S(1)} %all_gather.11), kind=kOutput, calls=%fused_computation.12 | convolution fusion | flops 151289856 | bytes 2555904 | tf_op jit(solution)/shard_map/hij,sjhe->sihe/dot_general | solution.py:54
  125.2 0.0 copy-start.5
  125.2 0.5 copy.14
  125.7 0.7 copy-done.5
  126.4 1.5 %convolution_convert_fusion = bf16[384,768]{1,0:T(8,128)(2,1)} fusion(bf16[768,768]{1,0:T(8,128)(2,1)S(1)} %copy-done.5, bf16[96,8,3,128]{3,2,1,0:T(4,128)(2,1)S(1)} %bitcast.31), kind=kOutput, calls=%fused_computation.7 | convolution fusion | flops 453279744 | bytes 2359296 | tf_op jit(solution)/shard_map/dot_general | solution.py:60
  (2 shorter events, 0.0 us)
Async XLA Ops:
  6.5 3.0 %copy-start = (bf16[768,768]{1,0:T(8,128)(2,1)S(1)}, bf16[768,768]{1,0:T(8,128)(2,1)}, u32[]{:S(2)}) copy-start(bf16[768,768]{1,0:T(8,128)(2,1)} %param.9) | copy-start | bytes 3538948
  6.5 2.8 %copy-start.1 = (bf16[3,128,768]{2,1,0:T(8,128)(2,1)S(1)}, bf16[3,128,768]{2,1,0:T(8,128)(2,1)}, u32[]{:S(2)}) copy-start(bf16[3,128,768]{2,1,0:T(8,128)(2,1)} %param.6) | copy-start | bytes 1769476
  6.5 2.8 %copy-start.2 = (f32[768]{0:T(1024)S(1)}, f32[768]{0:T(1024)}, u32[]{:S(2)}) copy-start(f32[768]{0:T(1024)} %param.7) | copy-start | bytes 9220
  6.5 30.4 %all-gather.5.cloned.1.call-start = ((), (), s32[]{:S(2)}) async-start(), calls=%async_computation.2 | async-start | bytes 1769472 | tf_op jit(solution)/shard_map/all_gather | solution.py:45
  10.2 1.5 %copy-start.3 = (bf16[768,768]{1,0:T(8,128)(2,1)S(1)}, bf16[768,768]{1,0:T(8,128)(2,1)}, u32[]{:S(2)}) copy-start(bf16[768,768]{1,0:T(8,128)(2,1)} %param.8) | copy-start | bytes 3538948
  11.3 88.8 %reduce-scatter.2.cloned.1.call-start = ((), (), s32[]{:S(2)}) async-start(), calls=%async_computation.3 | async-start | bytes 1671168 | tf_op jit(solution)/shard_map/reduce_scatter | solution.py:50
  39.8 1.3 copy-start.4
  39.8 83.6 %all-gather.3.cloned.1.call-start = ((), (), s32[]{:S(2)}) async-start(), calls=%async_computation.1 | async-start | bytes 1769472 | tf_op jit(solution)/shard_map/all_gather | solution.py:46
  125.2 1.3 copy-start.5
Sparse Core Ops, SparseCore 0:
  11.4 25.4 all-gather.4
  40.6 59.5 reduce-scatter.1
  101.7 21.6 all-gather.2
where the time goes:
time: 135 us; the launch traced here: 134 us
  waiting for transfers between devices  79.9 us (59%)
  blocking collectives  21.5 us (16%)
  between operations  13.2 us (10%)
  matrix products  8.81 us (7%)
  local copies, waits for them, and re-layouts  6.86 us (5%)
  other arithmetic  4.05 us (3%)
    reduce_scatter x1, waiting for transfers between devices, body(): share = lax.psum_scatter(logits, 'seq', scatter_dimension=1, tiled=True)  57.4 us
    all_gather x1, waiting for transfers between devices, body(): lax.all_gather(key_local, 'res', axis=1, tiled=True)  21.8 us
    all_gather x1, blocking collectives, body(): probs = lax.all_gather(share_probs, 'seq', axis=1, tiled=True)  21.5 us
    dot_general x1, matrix products, body(): jnp.einsum('sihe,sjhe->hij', query, keys, preferred_element_type=jnp.floa...  2.9 us
  transfers between devices with their start and end apart: 3, of which 3 were waited for; matrix products, arithmetic and copies ran while one was open for 5% of the time, Pallas kernels for 0%

commit v1 on v0

--- a/solution.py
+++ b/solution.py
@@ -49,7 +49,24 @@
     logits = jnp.einsum("sihe,sjhe->hij", query, keys, preferred_element_type=jnp.float32)
     share = lax.psum_scatter(logits, "seq", scatter_dimension=1, tiled=True)
     share_probs = jax.nn.softmax(share * scale, axis=-1).astype(jnp.bfloat16)
-    probs = lax.all_gather(share_probs, "seq", axis=1, tiled=True)
+
+    def _save_windows(load):
+        n_slots = lax.axis_size("seq")
+        ix = 0
+        trail = [load]
+        while ix < n_slots - 1:
+            block_now = lax.ppermute(
+                trail[-1],
+                axis_name="seq",
+                perm=[(dev, (dev + 1) % n_slots) for dev in range(n_slots)],
+            )
+            trail.append(block_now)
+            ix += 1
+        arr_now = jnp.concatenate(trail[::-1], axis=1)
+        current_block = lax.axis_index("seq")
+        return jnp.roll(arr_now, (current_block + 1) * load.shape[1], axis=1)
+
+    probs = _save_windows(share_probs)
     content_array = value_all.reshape(row_portion, value_all.shape[1], heads, hsize)
     attended = jnp.einsum(
         "hij,sjhe->sihe", probs, content_array, preferred_element_type=jnp.float32

time: 135 us -> 227 us (1.68)
  waiting for transfers between devices: 79.9 us -> 172 us
  blocking collectives: 21.5 us -> 0 us
  local copies, waits for them, and re-layouts: 6.86 us -> 23.5 us
  matrix products: 8.81 us -> 11.7 us
    ppermute x0 -> x15, waiting for transfers between devices: none -> 90.1 us  [_save_windows(): lax.ppermute(trail[-1], axis_name='seq', perm=[(dev, (dev + 1) % n_slots)...]
    all_gather x1 -> x0, blocking collectives: 21.5 us -> none  [body(): probs = lax.all_gather(share_probs, 'seq', axis=1, tiled=True)]
    unnamed x12 -> x36, local copies, waits for them, and re-layouts: 2.3 us -> 18.9 us
    reduce_scatter x1, waiting for transfers between devices: 57.4 us -> 60.3 us  [body(): share = lax.psum_scatter(logits, 'seq', scatter_dimension=1, tiled=True)]
  transfers between devices with their start and end apart: 3 -> 18, of which waited for: 3 -> 18; matrix products, arithmetic and copies ran while one was open for 5% -> 12% of each run, Pallas kernels for 0% -> 0%
where the time goes in v1:
time: 227 us
  waiting for transfers between devices  172 us (76%)
  local copies, waits for them, and re-layouts  23.5 us (10%)
  between operations  13.3 us (6%)
  matrix products  11.7 us (5%)
  other arithmetic  6.26 us (3%)
    ppermute x15, waiting for transfers between devices, _save_windows(): lax.ppermute(trail[-1], axis_name='seq', perm=[(dev, (dev + 1) % n_slots)...  90.1 us
    reduce_scatter x1, waiting for transfers between devices, body(): share = lax.psum_scatter(logits, 'seq', scatter_dimension=1, tiled=True)  60.3 us
    all_gather x1, waiting for transfers between devices, body(): lax.all_gather(key_local, 'res', axis=1, tiled=True)  20.9 us
    unnamed x36, local copies, waits for them, and re-layouts  18.9 us
  transfers between devices with their start and end apart: 18, of which 18 were waited for; matrix products, arithmetic and copies ran while one was open for 12% of the time, Pallas kernels for 0%

profile of v1, /device:TPU:0, one launch (start us, length us, event | category | flops | bytes accessed | tf_op | source)
XLA Modules:
  0.0 226.6 jit_solution(11769689773727919017)
XLA Ops:
  6.5 1.4 convert_reduce_fusion
  7.9 1.4 fusion.4
  9.3 0.9 fusion.6
  10.9 1.1 copy.10
  12.0 2.7 %convolution_convert_fusion.3 = bf16[384,768]{1,0:T(8,128)(2,1)} fusion(bf16[384,768]{1,0:T(8,128)(2,1)S(1)} %bitcast.33, bf16[768,768]{1,0:T(8,128)(2,1)} %param.8), kind=kOutput, calls=%fused_computation.9 | convolution fusion | flops 453279744 | bytes 2359296 | tf_op jit(solution)/shard_map/dot_general | solution.py:30
  14.7 1.9 reshape.49
  16.7 20.9 %all-gather.5.cloned.1.call-done = bf16[3,256,768]{1,2,0:T(8,128)(2,1)} async-done(((bf16[3,128,768]{1,2,0:T(8,128)(2,1)}), bf16[3,256,768]{1,2,0:T(8,128)(2,1)}) %all-gather.5.cloned.1.call-update) | async-done | bytes 1179664 | tf_op jit(solution)/shard_map/all_gather | solution.py:45
  37.6 2.9 %convolution_bitcast_fusion = f32[12,128,256]{2,1,0:T(8,128)} fusion(bf16[3,128,12,64]{3,2,1,0:T(8,128)(2,1)S(1)} %reshape.49, bf16[3,256,12,64]{1,3,2,0:T(8,128)(2,1)} %bitcast.30), kind=kOutput, calls=%fused_computation.1 | convolution fusion | flops 150994944 | bytes 3342336 | tf_op jit(solution)/shard_map/sihe,sjhe->hij/dot_general | solution.py:49
  40.5 60.3 %reduce-scatter.2.cloned.1.call-done = f32[12,8,256]{2,1,0:T(8,128)} async-done(((f32[12,128,256]{2,1,0:T(8,128)}), f32[12,8,256]{2,1,0:T(8,128)}) %reduce-scatter.2.cloned.1.call-update) | async-done | bytes 98320 | tf_op jit(solution)/shard_map/reduce_scatter | solution.py:50
  100.8 1.1 fusion.20
  102.0 6.2 %collective-permute-done = bf16[12,8,256]{2,1,0:T(8,128)(2,1)S(1)} collective-permute-done((bf16[12,8,256]{2,1,0:T(8,128)(2,1)S(1)}, bf16[12,8,256]{2,1,0:T(8,128)(2,1)S(1)}, u32[]{:S(2)}, u32[]{:S(2)}) %collective-permute-start) | collective-permute-done | bytes 49184 | tf_op jit(solution)/shard_map/ppermute | solution.py:58
  108.2 6.2 %collective-permute-done.1 = bf16[12,8,256]{2,1,0:T(8,128)(2,1)S(1)} collective-permute-done((bf16[12,8,256]{2,1,0:T(8,128)(2,1)S(1)}, bf16[12,8,256]{2,1,0:T(8,128)(2,1)S(1)}, u32[]{:S(2)}, u32[]{:S(2)}) %collective-permute-start.1) | collective-permute-done | bytes 49184 | tf_op jit(solution)/shard_map/ppermute | solution.py:58
  114.4 6.2 %collective-permute-done.2 = bf16[12,8,256]{2,1,0:T(8,128)(2,1)S(1)} collective-permute-done((bf16[12,8,256]{2,1,0:T(8,128)(2,1)S(1)}, bf16[12,8,256]{2,1,0:T(8,128)(2,1)S(1)}, u32[]{:S(2)}, u32[]{:S(2)}) %collective-permute-start.2) | collective-permute-done | bytes 49184 | tf_op jit(solution)/shard_map/ppermute | solution.py:58
  120.7 6.2 %collective-permute-done.3 = bf16[12,8,256]{2,1,0:T(8,128)(2,1)S(1)} collective-permute-done((bf16[12,8,256]{2,1,0:T(8,128)(2,1)S(1)}, bf16[12,8,256]{2,1,0:T(8,128)(2,1)S(1)}, u32[]{:S(2)}, u32[]{:S(2)}) %collective-permute-start.3) | collective-permute-done | bytes 49184 | tf_op jit(solution)/shard_map/ppermute | solution.py:58
  126.9 6.2 %collective-permute-done.4 = bf16[12,8,256]{2,1,0:T(8,128)(2,1)S(1)} collective-permute-done((bf16[12,8,256]{2,1,0:T(8,128)(2,1)S(1)}, bf16[12,8,256]{2,1,0:T(8,128)(2,1)S(1)}, u32[]{:S(2)}, u32[]{:S(2)}) %collective-permute-start.4) | collective-permute-done | bytes 49184 | tf_op jit(solution)/shard_map/ppermute | solution.py:58
  133.1 6.2 %collective-permute-done.5 = bf16[12,8,256]{2,1,0:T(8,128)(2,1)S(1)} collective-permute-done((bf16[12,8,256]{2,1,0:T(8,128)(2,1)S(1)}, bf16[12,8,256]{2,1,0:T(8,128)(2,1)S(1)}, u32[]{:S(2)}, u32[]{:S(2)}) %collective-permute-start.5) | collective-permute-done | bytes 49184 | tf_op jit(solution)/shard_map/ppermute | solution.py:58
  139.3 6.2 %collective-permute-done.6 = bf16[12,8,256]{2,1,0:T(8,128)(2,1)S(1)} collective-permute-done((bf16[12,8,256]{2,1,0:T(8,128)(2,1)S(1)}, bf16[12,8,256]{2,1,0:T(8,128)(2,1)S(1)}, u32[]{:S(2)}, u32[]{:S(2)}) %collective-permute-start.6) | collective-permute-done | bytes 49184 | tf_op jit(solution)/shard_map/ppermute | solution.py:58
  145.5 6.2 %collective-permute-done.7 = bf16[12,8,256]{2,1,0:T(8,128)(2,1)S(1)} collective-permute-done((bf16[12,8,256]{2,1,0:T(8,128)(2,1)S(1)}, bf16[12,8,256]{2,1,0:T(8,128)(2,1)S(1)}, u32[]{:S(2)}, u32[]{:S(2)}) %collective-permute-start.7) | collective-permute-done | bytes 49184 | tf_op jit(solution)/shard_map/ppermute | solution.py:58
  151.7 6.2 %collective-permute-done.8 = bf16[12,8,256]{2,1,0:T(8,128)(2,1)S(1)} collective-permute-done((bf16[12,8,256]{2,1,0:T(8,128)(2,1)S(1)}, bf16[12,8,256]{2,1,0:T(8,128)(2,1)S(1)}, u32[]{:S(2)}, u32[]{:S(2)}) %collective-permute-start.8) | collective-permute-done | bytes 49184 | tf_op jit(solution)/shard_map/ppermute | solution.py:58
  157.9 6.2 %collective-permute-done.9 = bf16[12,8,256]{2,1,0:T(8,128)(2,1)S(1)} collective-permute-done((bf16[12,8,256]{2,1,0:T(8,128)(2,1)S(1)}, bf16[12,8,256]{2,1,0:T(8,128)(2,1)S(1)}, u32[]{:S(2)}, u32[]{:S(2)}) %collective-permute-start.9) | collective-permute-done | bytes 49184 | tf_op jit(solution)/shard_map/ppermute | solution.py:58
  164.1 6.2 %collective-permute-done.10 = bf16[12,8,256]{2,1,0:T(8,128)(2,1)S(1)} collective-permute-done((bf16[12,8,256]{2,1,0:T(8,128)(2,1)S(1)}, bf16[12,8,256]{2,1,0:T(8,128)(2,1)S(1)}, u32[]{:S(2)}, u32[]{:S(2)}) %collective-permute-start.10) | collective-permute-done | bytes 49184 | tf_op jit(solution)/shard_map/ppermute | solution.py:58
  170.4 6.2 %collective-permute-done.11 = bf16[12,8,256]{2,1,0:T(8,128)(2,1)S(1)} collective-permute-done((bf16[12,8,256]{2,1,0:T(8,128)(2,1)S(1)}, bf16[12,8,256]{2,1,0:T(8,128)(2,1)S(1)}, u32[]{:S(2)}, u32[]{:S(2)}) %collective-permute-start.11) | collective-permute-done | bytes 49184 | tf_op jit(solution)/shard_map/ppermute | solution.py:58
  176.6 6.2 %collective-permute-done.12 = bf16[12,8,256]{2,1,0:T(8,128)(2,1)S(1)} collective-permute-done((bf16[12,8,256]{2,1,0:T(8,128)(2,1)S(1)}, bf16[12,8,256]{2,1,0:T(8,128)(2,1)S(1)}, u32[]{:S(2)}, u32[]{:S(2)}) %collective-permute-start.12) | collective-permute-done | bytes 49184 | tf_op jit(solution)/shard_map/ppermute | solution.py:58
  182.8 6.2 %collective-permute-done.13 = bf16[12,8,256]{2,1,0:T(8,128)(2,1)S(1)} collective-permute-done((bf16[12,8,256]{2,1,0:T(8,128)(2,1)S(1)}, bf16[12,8,256]{2,1,0:T(8,128)(2,1)S(1)}, u32[]{:S(2)}, u32[]{:S(2)}) %collective-permute-start.13) | collective-permute-done | bytes 49184 | tf_op jit(solution)/shard_map/ppermute | solution.py:58
  189.0 1.9 convolution_convert_fusion.4
  190.9 1.1 copy.8
  192.0 3.2 %collective-permute-done.14 = bf16[12,8,256]{2,1,0:T(8,128)(2,1)S(1)} collective-permute-done((bf16[12,8,256]{2,1,0:T(8,128)(2,1)S(1)}, bf16[12,8,256]{2,1,0:T(8,128)(2,1)S(1)}, u32[]{:S(2)}, u32[]{:S(2)}) %collective-permute-start.14) | collective-permute-done | bytes 49184 | tf_op jit(solution)/shard_map/ppermute | solution.py:58
  195.8 0.6 constant_dynamic-update-slice_fusion.30
  197.1 0.6 constant_dynamic-update-slice_fusion.28
  199.0 0.6 constant_dynamic-update-slice_fusion.25
  200.2 0.6 constant_dynamic-update-slice_fusion.23
  200.9 0.6 constant_dynamic-update-slice_fusion.22
  201.5 0.7 constant_dynamic-update-slice_fusion.21
  202.2 0.6 constant_dynamic-update-slice_fusion.20
  202.8 0.6 constant_dynamic-update-slice_fusion.19
  203.4 0.6 constant_dynamic-update-slice_fusion.18
  204.1 0.6 constant_dynamic-update-slice_fusion.17
  204.7 0.7 constant_dynamic-update-slice_fusion.16
  205.4 0.6 constant_dynamic-update-slice_fusion.15
  206.1 0.6 constant_dynamic-update-slice_fusion.14
  207.9 0.6 constant_dynamic-update-slice_fusion.11
  208.6 0.6 constant_dynamic-update-slice_fusion.10
  209.8 0.6 constant_dynamic-update-slice_fusion.8
  212.3 0.6 constant_dynamic-update-slice_fusion.4
  214.2 0.6 constant_dynamic-update-slice_fusion.1
  214.9 0.7 constant_dynamic-update-slice_fusion
  216.0 2.0 fusion.3
  218.6 1.5 convolution_convert_fusion
  (46 shorter events, 10.0 us)
Async XLA Ops:
  6.5 3.7 %copy-start = (bf16[768,768]{1,0:T(8,128)(2,1)S(1)}, bf16[768,768]{1,0:T(8,128)(2,1)}, u32[]{:S(2)}) copy-start(bf16[768,768]{1,0:T(8,128)(2,1)} %param.9) | copy-start | bytes 3538948
  6.5 2.7 %copy-start.1 = (bf16[3,128,768]{2,1,0:T(8,128)(2,1)S(1)}, bf16[3,128,768]{2,1,0:T(8,128)(2,1)}, u32[]{:S(2)}) copy-start(bf16[3,128,768]{2,1,0:T(8,128)(2,1)} %param.6) | copy-start | bytes 1769476
  6.5 31.0 %all-gather.5.cloned.1.call-start = ((), (), s32[]{:S(2)}) async-start(), calls=%async_computation.2 | async-start | bytes 1769472 | tf_op jit(solution)/shard_map/all_gather | solution.py:45
  12.0 88.8 %reduce-scatter.2.cloned.1.call-start = ((), (), s32[]{:S(2)}) async-start(), calls=%async_computation.3 | async-start | bytes 1671168 | tf_op jit(solution)/shard_map/reduce_scatter | solution.py:50
  40.5 175.5 %all-gather.3.cloned.1.call-start = ((), (), s32[]{:S(2)}) async-start(), calls=%async_computation.1 | async-start | bytes 1769472 | tf_op jit(solution)/shard_map/all_gather | solution.py:46
  102.0 6.3 %collective-permute-start = (bf16[12,8,256]{2,1,0:T(8,128)(2,1)S(1)}, bf16[12,8,256]{2,1,0:T(8,128)(2,1)S(1)}, u32[]{:S(2)}, u32[]{:S(2)}) collective-permute-start(bf16[12,8,256]{2,1,0:T(8,128)(2,1)S(1)} %divide_convert_fusion), channel_id=1, source_target_pairs={{0,2},{2,4},{4,6},{6,8},{8,10},{10,12},{12,14},{14,16},{16,18},{18... | collective-permute-start | bytes 147464 | tf_op jit(solution)/shard_map/ppermute | solution.py:58
  108.2 6.2 %collective-permute-start.1 = (bf16[12,8,256]{2,1,0:T(8,128)(2,1)S(1)}, bf16[12,8,256]{2,1,0:T(8,128)(2,1)S(1)}, u32[]{:S(2)}, u32[]{:S(2)}) collective-permute-start(bf16[12,8,256]{2,1,0:T(8,128)(2,1)S(1)} %collective-permute-done), channel_id=1, source_target_pairs={{0,2},{2,4},{4,6},{6,8},{8,10},{10,12},{12,14},{14,16},{16,18},{18... | collective-permute-start | bytes 147464 | tf_op jit(solution)/shard_map/ppermute | solution.py:58
  114.4 6.2 %collective-permute-start.2 = (bf16[12,8,256]{2,1,0:T(8,128)(2,1)S(1)}, bf16[12,8,256]{2,1,0:T(8,128)(2,1)S(1)}, u32[]{:S(2)}, u32[]{:S(2)}) collective-permute-start(bf16[12,8,256]{2,1,0:T(8,128)(2,1)S(1)} %collective-permute-done.1), channel_id=1, source_target_pairs={{0,2},{2,4},{4,6},{6,8},{8,10},{10,12},{12,14},{14,16},{16,18},{18... | collective-permute-start | bytes 147464 | tf_op jit(solution)/shard_map/ppermute | solution.py:58
  120.6 6.2 %collective-permute-start.3 = (bf16[12,8,256]{2,1,0:T(8,128)(2,1)S(1)}, bf16[12,8,256]{2,1,0:T(8,128)(2,1)S(1)}, u32[]{:S(2)}, u32[]{:S(2)}) collective-permute-start(bf16[12,8,256]{2,1,0:T(8,128)(2,1)S(1)} %collective-permute-done.2), channel_id=1, source_target_pairs={{0,2},{2,4},{4,6},{6,8},{8,10},{10,12},{12,14},{14,16},{16,18},{18... | collective-permute-start | bytes 147464 | tf_op jit(solution)/shard_map/ppermute | solution.py:58
  126.9 6.2 %collective-permute-start.4 = (bf16[12,8,256]{2,1,0:T(8,128)(2,1)S(1)}, bf16[12,8,256]{2,1,0:T(8,128)(2,1)S(1)}, u32[]{:S(2)}, u32[]{:S(2)}) collective-permute-start(bf16[12,8,256]{2,1,0:T(8,128)(2,1)S(1)} %collective-permute-done.3), channel_id=1, source_target_pairs={{0,2},{2,4},{4,6},{6,8},{8,10},{10,12},{12,14},{14,16},{16,18},{18... | collective-permute-start | bytes 147464 | tf_op jit(solution)/shard_map/ppermute | solution.py:58
  133.1 6.2 %collective-permute-start.5 = (bf16[12,8,256]{2,1,0:T(8,128)(2,1)S(1)}, bf16[12,8,256]{2,1,0:T(8,128)(2,1)S(1)}, u32[]{:S(2)}, u32[]{:S(2)}) collective-permute-start(bf16[12,8,256]{2,1,0:T(8,128)(2,1)S(1)} %collective-permute-done.4), channel_id=1, source_target_pairs={{0,2},{2,4},{4,6},{6,8},{8,10},{10,12},{12,14},{14,16},{16,18},{18... | collective-permute-start | bytes 147464 | tf_op jit(solution)/shard_map/ppermute | solution.py:58
  139.3 6.2 %collective-permute-start.6 = (bf16[12,8,256]{2,1,0:T(8,128)(2,1)S(1)}, bf16[12,8,256]{2,1,0:T(8,128)(2,1)S(1)}, u32[]{:S(2)}, u32[]{:S(2)}) collective-permute-start(bf16[12,8,256]{2,1,0:T(8,128)(2,1)S(1)} %collective-permute-done.5), channel_id=1, source_target_pairs={{0,2},{2,4},{4,6},{6,8},{8,10},{10,12},{12,14},{14,16},{16,18},{18... | collective-permute-start | bytes 147464 | tf_op jit(solution)/shard_map/ppermute | solution.py:58
  145.5 6.2 %collective-permute-start.7 = (bf16[12,8,256]{2,1,0:T(8,128)(2,1)S(1)}, bf16[12,8,256]{2,1,0:T(8,128)(2,1)S(1)}, u32[]{:S(2)}, u32[]{:S(2)}) collective-permute-start(bf16[12,8,256]{2,1,0:T(8,128)(2,1)S(1)} %collective-permute-done.6), channel_id=1, source_target_pairs={{0,2},{2,4},{4,6},{6,8},{8,10},{10,12},{12,14},{14,16},{16,18},{18... | collective-permute-start | bytes 147464 | tf_op jit(solution)/shard_map/ppermute | solution.py:58
  151.7 6.2 %collective-permute-start.8 = (bf16[12,8,256]{2,1,0:T(8,128)(2,1)S(1)}, bf16[12,8,256]{2,1,0:T(8,128)(2,1)S(1)}, u32[]{:S(2)}, u32[]{:S(2)}) collective-permute-start(bf16[12,8,256]{2,1,0:T(8,128)(2,1)S(1)} %collective-permute-done.7), channel_id=1, source_target_pairs={{0,2},{2,4},{4,6},{6,8},{8,10},{10,12},{12,14},{14,16},{16,18},{18... | collective-permute-start | bytes 147464 | tf_op jit(solution)/shard_map/ppermute | solution.py:58
  157.9 6.2 %collective-permute-start.9 = (bf16[12,8,256]{2,1,0:T(8,128)(2,1)S(1)}, bf16[12,8,256]{2,1,0:T(8,128)(2,1)S(1)}, u32[]{:S(2)}, u32[]{:S(2)}) collective-permute-start(bf16[12,8,256]{2,1,0:T(8,128)(2,1)S(1)} %collective-permute-done.8), channel_id=1, source_target_pairs={{0,2},{2,4},{4,6},{6,8},{8,10},{10,12},{12,14},{14,16},{16,18},{18... | collective-permute-start | bytes 147464 | tf_op jit(solution)/shard_map/ppermute | solution.py:58
  164.1 6.2 %collective-permute-start.10 = (bf16[12,8,256]{2,1,0:T(8,128)(2,1)S(1)}, bf16[12,8,256]{2,1,0:T(8,128)(2,1)S(1)}, u32[]{:S(2)}, u32[]{:S(2)}) collective-permute-start(bf16[12,8,256]{2,1,0:T(8,128)(2,1)S(1)} %collective-permute-done.9), channel_id=1, source_target_pairs={{0,2},{2,4},{4,6},{6,8},{8,10},{10,12},{12,14},{14,16},{16,18},{18... | collective-permute-start | bytes 147464 | tf_op jit(solution)/shard_map/ppermute | solution.py:58
  170.3 6.2 %collective-permute-start.11 = (bf16[12,8,256]{2,1,0:T(8,128)(2,1)S(1)}, bf16[12,8,256]{2,1,0:T(8,128)(2,1)S(1)}, u32[]{:S(2)}, u32[]{:S(2)}) collective-permute-start(bf16[12,8,256]{2,1,0:T(8,128)(2,1)S(1)} %collective-permute-done.10), channel_id=1, source_target_pairs={{0,2},{2,4},{4,6},{6,8},{8,10},{10,12},{12,14},{14,16},{16,18},{18... | collective-permute-start | bytes 147464 | tf_op jit(solution)/shard_map/ppermute | solution.py:58
  176.6 6.2 %collective-permute-start.12 = (bf16[12,8,256]{2,1,0:T(8,128)(2,1)S(1)}, bf16[12,8,256]{2,1,0:T(8,128)(2,1)S(1)}, u32[]{:S(2)}, u32[]{:S(2)}) collective-permute-start(bf16[12,8,256]{2,1,0:T(8,128)(2,1)S(1)} %collective-permute-done.11), channel_id=1, source_target_pairs={{0,2},{2,4},{4,6},{6,8},{8,10},{10,12},{12,14},{14,16},{16,18},{18... | collective-permute-start | bytes 147464 | tf_op jit(solution)/shard_map/ppermute | solution.py:58
  182.8 6.2 %collective-permute-start.13 = (bf16[12,8,256]{2,1,0:T(8,128)(2,1)S(1)}, bf16[12,8,256]{2,1,0:T(8,128)(2,1)S(1)}, u32[]{:S(2)}, u32[]{:S(2)}) collective-permute-start(bf16[12,8,256]{2,1,0:T(8,128)(2,1)S(1)} %collective-permute-done.12), channel_id=1, source_target_pairs={{0,2},{2,4},{4,6},{6,8},{8,10},{10,12},{12,14},{14,16},{16,18},{18... | collective-permute-start | bytes 147464 | tf_op jit(solution)/shard_map/ppermute | solution.py:58
  189.0 6.2 %collective-permute-start.14 = (bf16[12,8,256]{2,1,0:T(8,128)(2,1)S(1)}, bf16[12,8,256]{2,1,0:T(8,128)(2,1)S(1)}, u32[]{:S(2)}, u32[]{:S(2)}) collective-permute-start(bf16[12,8,256]{2,1,0:T(8,128)(2,1)S(1)} %collective-permute-done.13), channel_id=1, source_target_pairs={{0,2},{2,4},{4,6},{6,8},{8,10},{10,12},{12,14},{14,16},{16,18},{18... | collective-permute-start | bytes 147464 | tf_op jit(solution)/shard_map/ppermute | solution.py:58
  216.0 2.6 %copy-start.2 = (bf16[768,768]{1,0:T(8,128)(2,1)S(1)}, bf16[768,768]{1,0:T(8,128)(2,1)}, u32[]{:S(2)}) copy-start(bf16[768,768]{1,0:T(8,128)(2,1)} %param.11) | copy-start | bytes 3538948
Sparse Core Ops, SparseCore 0:
  12.1 25.4 all-gather.4
  41.2 59.5 reduce-scatter.1
  192.1 23.8 all-gather.2
